TPU v7x, 256 devices: a whole 4x4x8 slice. The times are simulated.
256 devices in a mesh: layer: 4 (over y), front: 64 (over z, x, core).
Axes of the slice: x: 4, y: 4, z: 8, core: 2. Of those that a mesh axis runs over, the one named last changes fastest.
Arguments:
- right_sides: float32 [4, 2, 4, 8192], P('layer', None, None, 'front'), may hold values from -6 to 6
- leaf_inverse: bfloat16 [4, 2, 8192, 128], P('layer', None, 'front'), may hold values from -0.375 to 0.375
- couple_above: bfloat16 [4, 2, 8192, 128], P('layer', None, 'front'), may hold values from -0.1875 to 0.1875
- couple_below: bfloat16 [4, 2, 8192, 128], P('layer', None, 'front'), may hold values from -0.1875 to 0.1875
- sep_gather: bfloat16 [4, 2, 5120, 8192], P('layer', None, None, 'front'), may hold values from -0.046875 to 0.046875
- sep_inverse: bfloat16 [4, 2, 5120, 5120], P('layer', None, 'front'), may hold values from -0.0625 to 0.0625
- sep_spread: bfloat16 [4, 2, 8192, 5120], P('layer', None, 'front'), may hold values from -0.0625 to 0.0625
- panel_owner: int32 [4, 64], P('layer'), may hold values from 0 to 63, each once within a row
Outputs:
- solution: float32 [4, 2, 4, 8192], P('layer', None, None, 'front')
Inputs may be any that keep to these rules, and one draw needn't show every extreme that they name: Each row of panel_owner names every slot 0 to 63 once.
All inputs are finite; a program needn't handle non-finite values.
Results may differ from a plain program's by a relative error of at most 0.023.
Values may be sent and summed in bfloat16 or wider, within the bound.
A program may use at most 128 MiB of HBM per device.

v0:
```python
import jax
import jax.numpy as jnp
from jax import lax
from jax.sharding import PartitionSpec as P


def from_behind(block, axis, distance):
    devices = range(lax.axis_size(axis))
    route = [(i - distance, i) for i in devices if i - distance in devices]
    return lax.ppermute(block, axis, route)


def dense_apply(matrix, vector):

    def single(left, right):
        return jnp.dot(right, left.T, preferred_element_type=jnp.float32)

    real_part = single(matrix[0], vector[0]) - single(matrix[1], vector[1])
    imag_part = single(matrix[0], vector[1]) + single(matrix[1], vector[0])
    return jnp.stack([real_part, imag_part])


def layer_solve(source, leaf, gather_map, sep_panel, spread, owner_row):
    leaf_values = dense_apply(leaf, source.astype(jnp.bfloat16))
    partial_sums = dense_apply(gather_map, leaf_values.astype(jnp.bfloat16))
    sep_rounded = lax.psum(partial_sums, "front").astype(jnp.bfloat16)
    own_rows = dense_apply(sep_panel, sep_rounded).astype(jnp.bfloat16)
    stored = lax.all_gather(own_rows, "front", axis=2, tiled=True)
    count = stored.shape[1]
    panels = stored.reshape(2, count, owner_row.shape[0], own_rows.shape[2])
    sep_values = jnp.take(panels, owner_row, axis=2).reshape(2, count, stored.shape[2])
    return leaf_values - dense_apply(spread, sep_values)


def local(
    right_sides,
    leaf_inverse,
    couple_above,
    couple_below,
    sep_gather,
    sep_inverse,
    sep_spread,
    panel_owner,
):
    depth = lax.axis_size("layer")
    owner_row = panel_owner[0]
    sources = right_sides[0]

    def solve(source):
        return layer_solve(
            source, leaf_inverse[0], sep_gather[0], sep_inverse[0], sep_spread[0], owner_row
        )

    forward = solve(sources)
    for step_index in range(depth - 1):
        from_prev = from_behind(forward.astype(jnp.bfloat16), "layer", 1)
        forward = solve(sources - dense_apply(couple_above[0], from_prev))
    solution = forward
    for step_index in range(depth - 1):
        from_next = from_behind(solution.astype(jnp.bfloat16), "layer", -1)
        solution = forward - solve(dense_apply(couple_below[0], from_next))
    return solution[None]


def solution(mesh):
    return jax.shard_map(
        local,
        mesh=mesh,
        in_specs=(
            P("layer", None, None, "front"),
            P("layer", None, "front", None),
            P("layer", None, "front", None),
            P("layer", None, "front", None),
            P("layer", None, None, "front"),
            P("layer", None, "front", None),
            P("layer", None, "front", None),
            P("layer", None),
        ),
        out_specs=P("layer", None, None, "front"),
        check_vma=False,
    )
```

profile of v0, /device:TPU:1, one launch (start us, length us, event | category | flops | bytes accessed | tf_op | source)
XLA Modules:
  0.0 2287.0 jit_solution(15067838010511855414)
XLA Ops:
  3.9 0.9 fusion.204
  5.8 1.8 fusion.108
  7.5 1.8 fusion.110
  10.3 249.5 %all-reduce.7 = bf16[2,4,5120]{2,1,0:T(4,128)(2,1)S(1)} all-reduce(f32[2,4,5120]{2,1,0:T(4,128)S(1)} %pad_maximum_fusion), channel_id=1, replica_groups=mesh['layer'=4,'front'=64] {'front'}, use_global_device_ids=true, to_apply=%region_0.0 | all-reduce | flops 40960 | bytes 245760 | tf_op jit(solution)/shard_map/psum | solution.py:26
  259.8 1.6 fusion.280
  261.4 1.5 fusion.278
  263.7 58.7 %all_gather.21 = bf16[2,4,5120]{1,0,2:T(2,128)(2,1)} all-gather(bf16[2,4,80]{1,0,2:T(2,128)(2,1)S(1)} %copy.58), channel_id=1, replica_groups=mesh['layer'=4,'front'=64] {'front'}, dimensions={2}, use_global_device_ids=true | all-gather | bytes 83200 | tf_op jit(solution)/shard_map/all_gather | solution.py:28
  322.4 5.4 copy.60
  329.1 1.9 fusion.40
  331.0 1.8 fusion.38
  333.7 3.2 collective-permute-start
  340.8 243.3 %all-reduce.8 = bf16[2,4,5120]{2,1,0:T(4,128)(2,1)S(1)} all-reduce(f32[2,4,5120]{2,1,0:T(4,128)S(1)} %pad_maximum_fusion.1), channel_id=1, replica_groups=mesh['layer'=4,'front'=64] {'front'}, use_global_device_ids=true, to_apply=%region_1.0 | all-reduce | flops 40960 | bytes 245760 | tf_op jit(solution)/shard_map/psum | solution.py:26
  584.1 1.6 fusion.276
  585.7 1.5 fusion.274
  588.0 59.3 %all_gather.22 = bf16[2,4,5120]{1,0,2:T(2,128)(2,1)} all-gather(bf16[2,4,80]{1,0,2:T(2,128)(2,1)S(1)} %copy.63), channel_id=1, replica_groups=mesh['layer'=4,'front'=64] {'front'}, dimensions={2}, use_global_device_ids=true | all-gather | bytes 83200 | tf_op jit(solution)/shard_map/all_gather | solution.py:28
  647.2 5.4 copy.65
  653.7 1.8 fusion.36
  655.7 1.9 fusion.34
  657.6 1.8 fusion.127
  659.8 3.6 collective-permute-start.1
  667.2 243.3 %all-reduce.9 = bf16[2,4,5120]{2,1,0:T(4,128)(2,1)S(1)} all-reduce(f32[2,4,5120]{2,1,0:T(4,128)S(1)} %pad_maximum_fusion.2), channel_id=1, replica_groups=mesh['layer'=4,'front'=64] {'front'}, use_global_device_ids=true, to_apply=%region_2.4 | all-reduce | flops 40960 | bytes 245760 | tf_op jit(solution)/shard_map/psum | solution.py:26
  910.5 1.6 fusion.272
  912.1 1.5 fusion.270
  914.4 58.7 %all_gather.23 = bf16[2,4,5120]{1,0,2:T(2,128)(2,1)} all-gather(bf16[2,4,80]{1,0,2:T(2,128)(2,1)S(1)} %copy.68), channel_id=1, replica_groups=mesh['layer'=4,'front'=64] {'front'}, dimensions={2}, use_global_device_ids=true | all-gather | bytes 83200 | tf_op jit(solution)/shard_map/all_gather | solution.py:28
  973.1 5.4 copy.70
  979.6 1.8 fusion.32
  981.6 1.9 fusion.30
  983.5 1.8 fusion.139
  985.7 3.6 collective-permute-start.2
  993.1 243.5 %all-reduce.10 = bf16[2,4,5120]{2,1,0:T(4,128)(2,1)S(1)} all-reduce(f32[2,4,5120]{2,1,0:T(4,128)S(1)} %pad_maximum_fusion.3), channel_id=1, replica_groups=mesh['layer'=4,'front'=64] {'front'}, use_global_device_ids=true, to_apply=%region_3.5 | all-reduce | flops 40960 | bytes 245760 | tf_op jit(solution)/shard_map/psum | solution.py:26
  1236.6 1.6 fusion.268
  1238.2 1.5 fusion.266
  1240.5 58.7 %all_gather.24 = bf16[2,4,5120]{1,0,2:T(2,128)(2,1)} all-gather(bf16[2,4,80]{1,0,2:T(2,128)(2,1)S(1)} %copy.73), channel_id=1, replica_groups=mesh['layer'=4,'front'=64] {'front'}, dimensions={2}, use_global_device_ids=true | all-gather | bytes 83200 | tf_op jit(solution)/shard_map/all_gather | solution.py:28
  1299.2 5.4 copy.75
  1305.7 1.8 fusion.28
  1307.7 1.9 fusion.26
  1309.6 1.8 fusion.148
  1311.9 1.3 collective-permute-start.3
  1313.2 3.3 collective-permute-done.3
  1319.5 243.3 %all-reduce.11 = bf16[2,4,5120]{2,1,0:T(4,128)(2,1)S(1)} all-reduce(f32[2,4,5120]{2,1,0:T(4,128)S(1)} %pad_maximum_fusion.4), channel_id=1, replica_groups=mesh['layer'=4,'front'=64] {'front'}, use_global_device_ids=true, to_apply=%region_4.6 | all-reduce | flops 40960 | bytes 245760 | tf_op jit(solution)/shard_map/psum | solution.py:26
  1562.8 1.6 fusion.264
  1564.4 1.5 fusion.262
  1566.7 58.7 %all_gather.25 = bf16[2,4,5120]{1,0,2:T(2,128)(2,1)} all-gather(bf16[2,4,80]{1,0,2:T(2,128)(2,1)S(1)} %copy.78), channel_id=1, replica_groups=mesh['layer'=4,'front'=64] {'front'}, dimensions={2}, use_global_device_ids=true | all-gather | bytes 83200 | tf_op jit(solution)/shard_map/all_gather | solution.py:28
  1625.4 5.4 copy.80
  1631.9 1.8 fusion.24
  1633.9 1.9 fusion.22
  1635.8 1.8 fusion.157
  1638.0 1.5 collective-permute-start.4
  1639.6 2.8 collective-permute-done.4
  1645.4 243.3 %all-reduce.12 = bf16[2,4,5120]{2,1,0:T(4,128)(2,1)S(1)} all-reduce(f32[2,4,5120]{2,1,0:T(4,128)S(1)} %pad_maximum_fusion.5), channel_id=1, replica_groups=mesh['layer'=4,'front'=64] {'front'}, use_global_device_ids=true, to_apply=%region_5.7 | all-reduce | flops 40960 | bytes 245760 | tf_op jit(solution)/shard_map/psum | solution.py:26
  1888.7 1.6 fusion.260
  1890.3 1.5 fusion.258
  1892.6 58.7 %all_gather.26 = bf16[2,4,5120]{1,0,2:T(2,128)(2,1)} all-gather(bf16[2,4,80]{1,0,2:T(2,128)(2,1)S(1)} %copy.83), channel_id=1, replica_groups=mesh['layer'=4,'front'=64] {'front'}, dimensions={2}, use_global_device_ids=true | all-gather | bytes 83200 | tf_op jit(solution)/shard_map/all_gather | solution.py:28
  1951.3 5.4 copy.85
  1957.9 1.8 fusion.20
  1959.8 1.9 fusion.18
  1961.7 1.8 fusion.169
  1964.0 1.3 collective-permute-start.5
  1965.3 3.0 collective-permute-done.5
  1971.3 243.4 %all-reduce.13 = bf16[2,4,5120]{2,1,0:T(4,128)(2,1)S(1)} all-reduce(f32[2,4,5120]{2,1,0:T(4,128)S(1)} %pad_maximum_fusion.6), channel_id=1, replica_groups=mesh['layer'=4,'front'=64] {'front'}, use_global_device_ids=true, to_apply=%region_6.8 | all-reduce | flops 40960 | bytes 245760 | tf_op jit(solution)/shard_map/psum | solution.py:26
  2214.8 1.5 fusion.256
  2216.2 1.5 fusion.254
  2218.5 59.0 %all_gather.27 = bf16[2,4,5120]{1,0,2:T(2,128)(2,1)} all-gather(bf16[2,4,80]{1,0,2:T(2,128)(2,1)S(1)} %copy.88), channel_id=1, replica_groups=mesh['layer'=4,'front'=64] {'front'}, dimensions={2}, use_global_device_ids=true | all-gather | bytes 83200 | tf_op jit(solution)/shard_map/all_gather | solution.py:28
  2277.5 5.5 copy.90
  (233 shorter events, 46.6 us)
Async XLA Ops:
  0.0 9.3 copy-start
  259.8 3.1 copy-start.12
  329.1 3.7 copy-start.1
  332.8 4.9 copy-start.9
  332.8 5.4 copy-start.11
  332.8 5.5 copy-start.8
  333.7 3.9 collective-permute-start
  584.1 3.1 copy-start.13
  655.6 3.7 copy-start.2
  659.8 4.3 collective-permute-start.1
  910.5 3.1 copy-start.14
  981.6 3.7 copy-start.3
  985.7 4.3 collective-permute-start.2
  1236.6 3.1 copy-start.15
  1307.7 3.7 copy-start.4
  1309.6 6.9 copy-start.10
  1311.9 4.6 collective-permute-start.3
  1562.8 3.1 copy-start.16
  1633.9 3.7 copy-start.5
  1638.0 4.3 collective-permute-start.4
  1888.7 3.1 copy-start.17
  1959.8 3.7 copy-start.6
  1964.0 4.3 collective-permute-start.5
  1971.3 246.4 %copy-start.18 = (bf16[1,2,80,5120]{3,2,1,0:T(8,128)(2,1)S(1)}, bf16[1,2,80,5120]{3,2,1,0:T(8,128)(2,1)}, u32[]{:S(2)}) copy-start(bf16[1,2,80,5120]{3,2,1,0:T(8,128)(2,1)} %param.15) | copy-start | bytes 4915204
  2277.5 6.7 copy-start.7
where the time goes:
time: 2300 us; the launch traced here: 2290 us
  blocking collectives  2120 us (92%)
  matrix products  87.5 us (4%)
  local copies, waits for them, and re-layouts  46.7 us (2%)
    psum x7, blocking collectives, layer_solve(): sep_rounded = lax.psum(partial_sums, 'front').astype(jnp.bfloat16)  1710 us
    all_gather x7, blocking collectives, layer_solve(): stored = lax.all_gather(own_rows, 'front', axis=2, tiled=True)  412 us
    dot_general x136, matrix products, single(): return jnp.dot(right, left.T, preferred_element_type=jnp.float32)  87.5 us
  transfers between devices with their start and end apart: 6, of which 6 were waited for; matrix products, arithmetic and copies ran while one was open for 0% of the time, Pallas kernels for 0%

commit v1 on v0

--- a/solution.py
+++ b/solution.py
@@ -2,6 +2,7 @@
 import jax.numpy as jnp
 from jax import lax
 from jax.sharding import PartitionSpec as P
+from jax.lax import all_gather
 
 
 def from_behind(block, axis, distance):
@@ -23,7 +24,8 @@
 def layer_solve(source, leaf, gather_map, sep_panel, spread, owner_row):
     leaf_values = dense_apply(leaf, source.astype(jnp.bfloat16))
     partial_sums = dense_apply(gather_map, leaf_values.astype(jnp.bfloat16))
-    sep_rounded = lax.psum(partial_sums, "front").astype(jnp.bfloat16)
+    _advance_keys = lambda xx, peer_axis: jnp.sum(all_gather(xx, peer_axis), axis=0)
+    sep_rounded = _advance_keys(partial_sums, "front").astype(jnp.bfloat16)
     own_rows = dense_apply(sep_panel, sep_rounded).astype(jnp.bfloat16)
     stored = lax.all_gather(own_rows, "front", axis=2, tiled=True)
     count = stored.shape[1]

time: 2300 us -> 1210 us (0.53)
  blocking collectives: 2120 us -> 384 us
  waiting for transfers between devices: 11.3 us -> 611 us
  other arithmetic: 4.45 us -> 50.4 us
    psum x7 -> x0, blocking collectives: 1710 us -> none  [layer_solve(): sep_rounded = lax.psum(partial_sums, 'front').astype(jnp.bfloat16)]
    all_gather x0 -> x7, waiting for transfers between devices: none -> 599 us  [layer_solve(): all_gather(xx, peer_axis)]
    reduce_sum x0 -> x7, other arithmetic: none -> 42.5 us  [layer_solve(): jnp.sum(all_gather(xx, peer_axis), axis=0)]
    all_gather x7, blocking collectives: 412 us -> 384 us  [layer_solve(): stored = lax.all_gather(own_rows, 'front', axis=2, tiled=True)]
  transfers between devices with their start and end apart: 6 -> 13, of which waited for: 6 -> 13; matrix products, arithmetic and copies ran while one was open for 0% -> 0% of each run, Pallas kernels for 0% -> 0%
where the time goes in v1:
time: 1210 us
  waiting for transfers between devices  611 us (50%)
  blocking collectives  384 us (32%)
  matrix products  85.3 us (7%)
  other arithmetic  50.4 us (4%)
  local copies, waits for them, and re-layouts  46.7 us (4%)
  between operations  14.7 us (1%)
  starting transfers between devices  13.7 us (1%)
    all_gather x7, waiting for transfers between devices, layer_solve(): all_gather(xx, peer_axis)  599 us
    all_gather x7, blocking collectives, layer_solve(): stored = lax.all_gather(own_rows, 'front', axis=2, tiled=True)  384 us
    dot_general x136, matrix products, single(): return jnp.dot(right, left.T, preferred_element_type=jnp.float32)  85.3 us
    reduce_sum x7, other arithmetic, layer_solve(): jnp.sum(all_gather(xx, peer_axis), axis=0)  42.5 us
    reshape x7, local copies, waits for them, and re-layouts, layer_solve(): panels = stored.reshape(2, count, owner_row.shape[0], own_rows.shape[2])  37.8 us
  transfers between devices with their start and end apart: 13, of which 13 were waited for; matrix products, arithmetic and copies ran while one was open for 0% of the time, Pallas kernels for 0%

profile of v1, /device:TPU:1, one launch (start us, length us, event | category | flops | bytes accessed | tf_op | source)
XLA Modules:
  0.0 1205.4 jit_solution(17404388164355153193)
XLA Ops:
  11.0 1.8 fusion.108
  12.8 1.8 fusion.110
  16.3 90.6 %all-gather.15.cloned.1.call-done = f32[128,4,5120]{2,1,0:T(4,128)} async-done(((f32[2,4,5120]{2,1,0:T(4,128)}), f32[128,4,5120]{2,1,0:T(4,128)}) %all-gather.15.cloned.1.call-update) | async-done | bytes 10485776 | tf_op jit(solution)/shard_map/all_gather | solution.py:27
  106.9 6.1 reduce_sum.63
  113.0 1.6 fusion.280
  114.6 1.5 fusion.278
  116.9 54.7 %all_gather.65 = bf16[2,4,5120]{1,0,2:T(2,128)(2,1)} all-gather(bf16[2,4,80]{1,0,2:T(2,128)(2,1)S(1)} %copy.58), channel_id=1, replica_groups=mesh['layer'=4,'front'=64] {'front'}, dimensions={2}, use_global_device_ids=true | all-gather | bytes 83200 | tf_op jit(solution)/shard_map/all_gather | solution.py:30
  171.5 5.4 copy.60
  178.2 1.9 fusion.40
  180.1 1.8 fusion.38
  182.8 3.1 collective-permute-start
  190.7 84.8 %all-gather.17.cloned.1.call-done = f32[128,4,5120]{2,1,0:T(4,128)} async-done(((f32[2,4,5120]{2,1,0:T(4,128)}), f32[128,4,5120]{2,1,0:T(4,128)}) %all-gather.17.cloned.1.call-update) | async-done | bytes 10485776 | tf_op jit(solution)/shard_map/all_gather | solution.py:27
  275.6 6.1 reduce_sum.64
  281.6 1.6 fusion.276
  283.2 1.5 fusion.274
  285.5 54.7 %all_gather.68 = bf16[2,4,5120]{1,0,2:T(2,128)(2,1)} all-gather(bf16[2,4,80]{1,0,2:T(2,128)(2,1)S(1)} %copy.63), channel_id=1, replica_groups=mesh['layer'=4,'front'=64] {'front'}, dimensions={2}, use_global_device_ids=true | all-gather | bytes 83200 | tf_op jit(solution)/shard_map/all_gather | solution.py:30
  340.2 5.4 copy.65
  346.7 1.8 fusion.36
  348.6 1.9 fusion.34
  350.5 1.8 fusion.127
  352.8 3.1 collective-permute-start.1
  360.4 85.0 %all-gather.19.cloned.1.call-done = f32[128,4,5120]{2,1,0:T(4,128)} async-done(((f32[2,4,5120]{2,1,0:T(4,128)}), f32[128,4,5120]{2,1,0:T(4,128)}) %all-gather.19.cloned.1.call-update) | async-done | bytes 10485776 | tf_op jit(solution)/shard_map/all_gather | solution.py:27
  445.5 6.1 reduce_sum.65
  451.5 1.6 fusion.272
  453.1 1.5 fusion.270
  455.4 55.1 %all_gather.71 = bf16[2,4,5120]{1,0,2:T(2,128)(2,1)} all-gather(bf16[2,4,80]{1,0,2:T(2,128)(2,1)S(1)} %copy.68), channel_id=1, replica_groups=mesh['layer'=4,'front'=64] {'front'}, dimensions={2}, use_global_device_ids=true | all-gather | bytes 83200 | tf_op jit(solution)/shard_map/all_gather | solution.py:30
  510.5 5.4 copy.70
  517.0 1.8 fusion.32
  519.0 1.9 fusion.30
  520.9 1.8 fusion.139
  523.1 3.1 collective-permute-start.2
  530.8 85.0 %all-gather.21.cloned.1.call-done = f32[128,4,5120]{2,1,0:T(4,128)} async-done(((f32[2,4,5120]{2,1,0:T(4,128)}), f32[128,4,5120]{2,1,0:T(4,128)}) %all-gather.21.cloned.1.call-update) | async-done | bytes 10485776 | tf_op jit(solution)/shard_map/all_gather | solution.py:27
  615.8 6.1 reduce_sum.66
  621.9 1.6 fusion.268
  625.7 54.8 %all_gather.74 = bf16[2,4,5120]{1,0,2:T(2,128)(2,1)} all-gather(bf16[2,4,80]{1,0,2:T(2,128)(2,1)S(1)} %copy.73), channel_id=1, replica_groups=mesh['layer'=4,'front'=64] {'front'}, dimensions={2}, use_global_device_ids=true | all-gather | bytes 83200 | tf_op jit(solution)/shard_map/all_gather | solution.py:30
  680.6 5.4 copy.75
  687.1 1.8 fusion.28
  689.0 1.9 fusion.26
  690.9 1.8 fusion.148
  694.5 3.0 collective-permute-done.3
  701.4 84.6 %all-gather.23.cloned.1.call-done = f32[128,4,5120]{2,1,0:T(4,128)} async-done(((f32[2,4,5120]{2,1,0:T(4,128)}), f32[128,4,5120]{2,1,0:T(4,128)}) %all-gather.23.cloned.1.call-update) | async-done | bytes 10485776 | tf_op jit(solution)/shard_map/all_gather | solution.py:27
  785.9 6.1 reduce_sum.67
  792.0 1.6 fusion.264
  793.6 1.5 fusion.262
  795.9 54.9 %all_gather.77 = bf16[2,4,5120]{1,0,2:T(2,128)(2,1)} all-gather(bf16[2,4,80]{1,0,2:T(2,128)(2,1)S(1)} %copy.78), channel_id=1, replica_groups=mesh['layer'=4,'front'=64] {'front'}, dimensions={2}, use_global_device_ids=true | all-gather | bytes 83200 | tf_op jit(solution)/shard_map/all_gather | solution.py:30
  850.7 5.4 copy.80
  857.3 1.8 fusion.24
  859.2 1.9 fusion.22
  861.1 1.8 fusion.157
  864.7 3.0 collective-permute-done.4
  871.5 84.6 %all-gather.25.cloned.1.call-done = f32[128,4,5120]{2,1,0:T(4,128)} async-done(((f32[2,4,5120]{2,1,0:T(4,128)}), f32[128,4,5120]{2,1,0:T(4,128)}) %all-gather.25.cloned.1.call-update) | async-done | bytes 10485776 | tf_op jit(solution)/shard_map/all_gather | solution.py:27
  956.1 6.1 reduce_sum.68
  962.1 1.6 fusion.260
  963.7 1.5 fusion.258
  966.0 54.9 %all_gather.80 = bf16[2,4,5120]{1,0,2:T(2,128)(2,1)} all-gather(bf16[2,4,80]{1,0,2:T(2,128)(2,1)S(1)} %copy.83), channel_id=1, replica_groups=mesh['layer'=4,'front'=64] {'front'}, dimensions={2}, use_global_device_ids=true | all-gather | bytes 83200 | tf_op jit(solution)/shard_map/all_gather | solution.py:30
  1020.9 5.4 copy.85
  1027.4 1.8 fusion.20
  1029.4 1.9 fusion.18
  1031.3 1.8 fusion.169
  1034.8 3.0 collective-permute-done.5
  1041.6 84.6 %all-gather.27.cloned.1.call-done = f32[128,4,5120]{2,1,0:T(4,128)} async-done(((f32[2,4,5120]{2,1,0:T(4,128)}), f32[128,4,5120]{2,1,0:T(4,128)}) %all-gather.27.cloned.1.call-update) | async-done | bytes 10485776 | tf_op jit(solution)/shard_map/all_gather | solution.py:27
  1126.2 6.2 reduce_sum.69
  1133.9 55.0 %all_gather.83 = bf16[2,4,5120]{1,0,2:T(2,128)(2,1)} all-gather(bf16[2,4,80]{1,0,2:T(2,128)(2,1)S(1)} %copy.88), channel_id=1, replica_groups=mesh['layer'=4,'front'=64] {'front'}, dimensions={2}, use_global_device_ids=true | all-gather | bytes 83200 | tf_op jit(solution)/shard_map/all_gather | solution.py:30
  1188.8 5.5 copy.90
  (256 shorter events, 57.6 us)
Async XLA Ops:
  6.5 8.0 copy-start
  6.5 100.4 %all-gather.15.cloned.1.call-start = ((), (), s32[]{:S(2)}) async-start(), calls=%async_computation | async-start | bytes 10649600 | tf_op jit(solution)/shard_map/all_gather | solution.py:27
  14.5 1.7 copy-start.19
  16.2 259.4 %all-gather.17.cloned.1.call-start = ((), (), s32[]{:S(2)}) async-start(), calls=%async_computation.1 | async-start | bytes 10649600 | tf_op jit(solution)/shard_map/all_gather | solution.py:27
  113.0 3.1 copy-start.12
  178.2 3.7 copy-start.1
  181.9 4.8 copy-start.9
  181.9 5.3 copy-start.11
  181.9 5.4 copy-start.8
  182.8 3.8 collective-permute-start
  190.5 255.0 %all-gather.19.cloned.1.call-start = ((), (), s32[]{:S(2)}) async-start(), calls=%async_computation.2 | async-start | bytes 10649600 | tf_op jit(solution)/shard_map/all_gather | solution.py:27
  281.6 3.1 copy-start.13
  348.6 3.7 copy-start.2
  352.8 3.8 collective-permute-start.1
  360.4 255.4 %all-gather.21.cloned.1.call-start = ((), (), s32[]{:S(2)}) async-start(), calls=%async_computation.3 | async-start | bytes 10649600 | tf_op jit(solution)/shard_map/all_gather | solution.py:27
  451.5 3.1 copy-start.14
  518.9 3.7 copy-start.3
  523.1 3.8 collective-permute-start.2
  530.7 255.2 %all-gather.23.cloned.1.call-start = ((), (), s32[]{:S(2)}) async-start(), calls=%async_computation.4 | async-start | bytes 10649600 | tf_op jit(solution)/shard_map/all_gather | solution.py:27
  621.9 3.1 copy-start.15
  689.0 3.7 copy-start.4
  690.9 6.6 copy-start.10
  693.2 4.3 collective-permute-start.3
  701.3 254.7 %all-gather.25.cloned.1.call-start = ((), (), s32[]{:S(2)}) async-start(), calls=%async_computation.5 | async-start | bytes 10649600 | tf_op jit(solution)/shard_map/all_gather | solution.py:27
  792.0 3.1 copy-start.16
  859.2 3.7 copy-start.5
  863.4 4.3 collective-permute-start.4
  871.5 254.8 %all-gather.27.cloned.1.call-start = ((), (), s32[]{:S(2)}) async-start(), calls=%async_computation.6 | async-start | bytes 10649600 | tf_op jit(solution)/shard_map/all_gather | solution.py:27
  962.1 3.1 copy-start.17
  1029.4 3.7 copy-start.6
  1033.5 4.3 collective-permute-start.5
  1126.2 6.2 copy-start.18
  1188.8 6.7 copy-start.7
Sparse Core Ops, SparseCore 0:
  16.3 90.5 all-gather.14
  190.6 84.9 all-gather.16
  360.5 84.9 all-gather.18
  530.8 84.9 all-gather.20
  701.4 84.4 all-gather.22
  871.6 84.4 all-gather.24
  1041.7 84.4 all-gather.26
